TPU v7x, 32 devices: a whole 2x2x4 slice. The times are simulated.
32 devices in a mesh: dp: 4 (over y, x), seq: 8 (over z, core).
Axes of the slice: x: 2, y: 2, z: 4, core: 2. Of those that a mesh axis runs over, the one named last changes fastest.
Arguments:
- tokens: float32 [4, 1024, 1024], P('dp', 'seq'), may hold values from -6 to 6
- cotangent: float32 [4, 1024, 1024], P('dp', 'seq'), may hold values from -6 to 6
- doc_ids: int32 [4, 1024], P('dp'), may hold values from 0 to 1, never falling along the last dimension, each value on 1 to 768 neighbouring positions
- in_weight: float32 [1024, 4384], P(('dp', 'seq')), may hold values from -0.1875 to 0.1875
- out_weight: float32 [1024, 2048], P(('dp', 'seq')), may hold values from -0.125 to 0.125
- in_m: float32 [1024, 4384], P(('dp', 'seq')), may hold values from -30 to 30
- in_v: float32 [1024, 4384], P(('dp', 'seq')), may hold values from 1 to 1000
- out_m: float32 [1024, 2048], P(('dp', 'seq')), may hold values from -30 to 30
- out_v: float32 [1024, 2048], P(('dp', 'seq')), may hold values from 1 to 1000
- vec_params: float32 [14688], replicated, as said below
- vec_m: float32 [14688], replicated, may hold values from -30 to 30
- vec_v: float32 [14688], replicated, may hold values from 1 to 1000
Outputs:
- activations: float32 [4, 1024, 1024], P('dp', 'seq')
- input_grad: float32 [4, 1024, 1024], P('dp', 'seq')
- in_grad: float32 [1024, 4384], P(('dp', 'seq'))
- out_grad: float32 [1024, 2048], P(('dp', 'seq'))
- vec_grad: float32 [14688], replicated
- in_new: float32 [1024, 4384], P(('dp', 'seq'))
- out_new: float32 [1024, 2048], P(('dp', 'seq'))
- vec_new: float32 [14688], replicated
- in_m_new: float32 [1024, 4384], P(('dp', 'seq'))
- in_v_new: float32 [1024, 4384], P(('dp', 'seq'))
- out_m_new: float32 [1024, 2048], P(('dp', 'seq'))
- out_v_new: float32 [1024, 2048], P(('dp', 'seq'))
- vec_m_new: float32 [14688], replicated
- vec_v_new: float32 [14688], replicated
Inputs may be any that keep to these rules, and one draw needn't show every extreme that they name: `doc_ids`: each row holds document 0 and then document 1, each of one or more positions, none longer than 768. `vec_params`: norm_gain and gate_gain lie in 0.7 to 1.3, skip_gain in 0.5 to 1.5, step_bias in -1 to 1, log_rate in -12 to -3.
All inputs are finite; a program needn't handle non-finite values.
Results may differ from a plain program's by a relative error of at most 0.015.
Values may be sent and summed in bfloat16 or wider, within the bound.
A program may use at most 192 MiB of HBM per device.

v0:
```python
import jax
import jax.numpy as jnp
from jax import lax
from jax.sharding import PartitionSpec as P

D = 1024
DI = 2048
H = 32
P_SIZE = 64
N = 128
KW = 4
STRETCH = 256
STEP = 10
CONV = 2304
norm_eps = 1e-05
beta_one = 0.9
beta_two = 0.95
learn_rate = 0.03
decay_rate = 0.1
adam_eps = 1e-08
top_precision = lax.Precision.HIGHEST


def shifted_2(block, axis, distance):
    devices = range(lax.axis_size(axis))
    route = [(i - distance, i) for i in devices if i - distance in devices]
    return lax.ppermute(block, axis, route)


def unpack(vector):
    cursor = D + DI
    norm_gain = vector[:D]
    gate_gain = vector[D:cursor]
    conv_kernel = vector[cursor : cursor + KW * CONV].reshape(KW, CONV)
    cursor = cursor + KW * CONV
    conv_bias = vector[cursor : cursor + CONV]
    cursor = cursor + CONV
    step_bias = vector[cursor : cursor + H]
    log_rate = vector[cursor + H : cursor + 2 * H]
    skip_gain = vector[cursor + 2 * H : cursor + 3 * H]
    return (norm_gain, gate_gain, conv_kernel, conv_bias, step_bias, log_rate, skip_gain)


def repack(norm_gain, gate_gain, conv_kernel, conv_bias, step_bias, log_rate, skip_gain):
    return jnp.concatenate(
        [norm_gain, gate_gain, conv_kernel.reshape(-1), conv_bias, step_bias, log_rate, skip_gain]
    )


def input_norm(inputs, gain):
    scale = lax.rsqrt(jnp.mean(inputs * inputs, axis=-1, keepdims=True) + norm_eps)
    return inputs * scale * gain[None, :]


def gate_norm(ssd_out, gate_in, gain):
    mixed = ssd_out * jax.nn.silu(gate_in)
    scale = lax.rsqrt(jnp.mean(mixed * mixed, axis=-1, keepdims=True) + norm_eps)
    return mixed * scale * gain[None, :]


def conv_silu(padded, conv_kernel, conv_bias, ext_ids):
    length = padded.shape[0] - (KW - 1)
    own_ids = ext_ids[KW - 1 :]
    total = jnp.zeros((length, padded.shape[1]), jnp.float32) + conv_bias[None, :]
    for offset in range(KW):
        valid = (ext_ids[offset : offset + length] == own_ids).astype(jnp.float32)
        total = (
            total + conv_kernel[offset][None, :] * padded[offset : offset + length] * valid[:, None]
        )
    return jax.nn.silu(total)


def rates(step_raw, step_bias, log_rate):
    step_size = jax.nn.softplus(step_raw + step_bias[None, :])
    log_decay = -jnp.exp(log_rate)[None, :] * step_size
    return (step_size, log_decay)


def ssd_block(state, pieces):
    values, input_map, output_map, step_size, log_decay, block_ids, prior_id = pieces
    length = values.shape[0]
    cumulative = jnp.cumsum(log_decay, axis=0)
    rows_index = lax.broadcasted_iota(jnp.int32, (length, length), 0)
    cols_index = lax.broadcasted_iota(jnp.int32, (length, length), 1)
    related = (block_ids[:, None] == block_ids[None, :]) & (rows_index >= cols_index)
    spans = cumulative.T[:, :, None] - cumulative.T[:, None, :]
    decays = jnp.where(related[None], jnp.exp(jnp.where(related[None], spans, 0.0)), 0.0)
    scores = jnp.dot(output_map, input_map.T, precision=top_precision)
    mixing = decays * scores[None] * step_size.T[:, None, :]
    inside = jnp.einsum("hij,jhp->ihp", mixing, values, precision=top_precision)
    carried = (block_ids == prior_id).astype(jnp.float32)
    reach = carried[:, None] * jnp.exp(cumulative)
    entering = (
        jnp.einsum("hpn,in->ihp", state, output_map, precision=top_precision) * reach[:, :, None]
    )
    ending = (block_ids == block_ids[-1]).astype(jnp.float32)
    tail_weight = ending[:, None] * jnp.exp(cumulative[-1][None, :] - cumulative) * step_size
    new_state = state * reach[-1][:, None, None] + jnp.einsum(
        "jh,jhp,jn->hpn", tail_weight, values, input_map, precision=top_precision
    )
    return (new_state, inside + entering)


def ssd_run(mixed_in, step_size, log_decay, skip_gain, row_ids, prior_id, state, block):
    length = mixed_in.shape[0]
    blocks = length // block
    values = mixed_in[:, :DI].reshape(length, H, P_SIZE)
    input_map = mixed_in[:, DI : DI + N]
    output_map = mixed_in[:, DI + N :]
    shifted = jnp.concatenate([jnp.reshape(prior_id, (1,)), row_ids[:-1]])
    priors = shifted.reshape(blocks, block)[:, 0]
    pieces = (
        values.reshape(blocks, block, H, P_SIZE),
        input_map.reshape(blocks, block, N),
        output_map.reshape(blocks, block, N),
        step_size.reshape(blocks, block, H),
        log_decay.reshape(blocks, block, H),
        row_ids.reshape(blocks, block),
        priors,
    )
    final, outputs = lax.scan(ssd_block, state, pieces)
    result = outputs.reshape(length, H, P_SIZE) + skip_gain[None, :, None] * values
    return (result.reshape(length, DI), final)


def adamw_update(param, grad, first, second):
    first_new = beta_one * first + (1.0 - beta_one) * grad
    second_new = beta_two * second + (1.0 - beta_two) * grad * grad
    corrected = first_new / (1.0 - beta_one**STEP)
    scaled = jnp.sqrt(second_new / (1.0 - beta_two**STEP)) + adam_eps
    return (
        param * (1.0 - learn_rate * decay_rate) - learn_rate * corrected / scaled,
        first_new,
        second_new,
    )


def body(
    tokens,
    cotangent,
    doc_ids,
    in_weight,
    out_weight,
    in_m,
    in_v,
    out_m,
    out_v,
    vec_params,
    vec_m,
    vec_v,
):
    in_work, out_work = (
        lax.all_gather(in_weight.astype(jnp.bfloat16), ("dp", "seq"), axis=0, tiled=True),
        lax.all_gather(out_weight.astype(jnp.bfloat16), ("dp", "seq"), axis=0, tiled=True),
    )
    norm_gain, gate_gain, conv_kernel, conv_bias, step_bias, log_rate, skip_gain = unpack(
        vec_params
    )
    inputs = tokens[0]
    upstream_f = cotangent[0]
    local_len = inputs.shape[0]
    block = min(STRETCH, local_len)
    padded_row = jnp.concatenate([jnp.full((KW - 1,), -1, jnp.int32), doc_ids[0]])
    offset = lax.axis_index("seq") * local_len
    ext_ids = lax.dynamic_slice_in_dim(padded_row, offset, local_len + KW - 1)
    own_ids = ext_ids[KW - 1 :]
    prior_id = ext_ids[KW - 2]
    zero_state = jnp.zeros((H, P_SIZE, N), jnp.float32)
    normed = input_norm(inputs, norm_gain).astype(jnp.bfloat16)
    projected = jnp.dot(normed, in_work, preferred_element_type=jnp.float32)
    gate_in = projected[:, :DI]
    conv_in = projected[:, DI : DI + CONV].astype(jnp.bfloat16)
    step_raw = projected[:, DI + CONV :]
    rim = shifted_2(conv_in[local_len - (KW - 1) :], "seq", 1)
    padded = lax.optimization_barrier(jnp.concatenate([rim, conv_in], axis=0)).astype(jnp.float32)
    mixed_in = lax.optimization_barrier(
        conv_silu(padded, conv_kernel, conv_bias, ext_ids).astype(jnp.bfloat16)
    ).astype(jnp.float32)
    output_map = mixed_in[:, DI + N :]

    def pre_chain(mixed, raw, bias_in, rate_in, skip_in):
        step_size, log_decay = rates(raw, bias_in, rate_in)
        local_out, local_state = ssd_run(
            mixed, step_size, log_decay, skip_in, own_ids, prior_id, zero_state, block
        )
        cumulative = jnp.cumsum(log_decay, axis=0)
        reach = (own_ids == prior_id).astype(jnp.float32)[:, None] * jnp.exp(cumulative)
        return (local_out, local_state, reach)

    local_out, local_state, reach = pre_chain(mixed_in, step_raw, step_bias, log_rate, skip_gain)
    decay = reach[-1]

    def relay(turn, entry_now):
        return shifted_2(decay[:, None, None] * entry_now + local_state, "seq", 1)

    entry = lax.fori_loop(0, lax.axis_size("seq") - 1, relay, zero_state)
    entering = (
        jnp.einsum("hpn,tn->thp", entry, output_map, precision=top_precision) * reach[:, :, None]
    )
    ssd_out = local_out + entering.reshape(local_len, DI)
    gated, gate_back = jax.vjp(gate_norm, ssd_out, gate_in, gate_gain)
    normed_out = gated.astype(jnp.bfloat16)
    outputs = inputs + lax.dot_general(
        normed_out, out_work, (((1,), (1,)), ((), ())), preferred_element_type=jnp.float32
    )
    upstream = upstream_f.astype(jnp.bfloat16)
    grad_gated = jnp.dot(upstream, out_work, preferred_element_type=jnp.float32)
    grad_ssd, grad_gate_in, grad_gate_gain = gate_back(grad_gated)
    own_part = jnp.einsum(
        "th,thp,tn->hpn",
        reach,
        grad_ssd.reshape(local_len, H, P_SIZE),
        output_map,
        precision=top_precision,
    )

    def back_relay(turn, later):
        return shifted_2(
            (own_part + decay[:, None, None] * later).astype(jnp.bfloat16), "seq", -1
        ).astype(jnp.float32)

    after = lax.fori_loop(0, lax.axis_size("seq") - 1, back_relay, zero_state)

    def complete(mixed, raw, bias_in, rate_in, skip_in):
        part_out, part_state, part_reach = pre_chain(mixed, raw, bias_in, rate_in, skip_in)
        reader = mixed[:, DI + N :]
        arriving = (
            jnp.einsum("hpn,tn->thp", entry, reader, precision=top_precision)
            * part_reach[:, :, None]
        )
        return (part_out + arriving.reshape(local_len, DI), part_reach[-1], part_state)

    _, ssd_back = jax.vjp(complete, mixed_in, step_raw, step_bias, log_rate, skip_gain)
    grad_mixed, grad_raw, grad_bias, grad_rate, grad_skip = ssd_back(
        (grad_ssd, jnp.sum(after * entry, axis=(1, 2)), after)
    )
    _, conv_back = jax.vjp(
        lambda values, kernel, constant: conv_silu(values, kernel, constant, ext_ids),
        padded,
        conv_kernel,
        conv_bias,
    )
    grad_padded, grad_kernel, grad_cbias = conv_back(grad_mixed)
    returned = shifted_2(grad_padded[: KW - 1], "seq", -1)
    grad_conv = jnp.concatenate(
        [grad_padded[KW - 1 : local_len], grad_padded[local_len:] + returned], axis=0
    )
    grad_proj = jnp.concatenate([grad_gate_in, grad_conv, grad_raw], axis=1).astype(jnp.bfloat16)
    grad_normed = lax.dot_general(
        grad_proj, in_work, (((1,), (1,)), ((), ())), preferred_element_type=jnp.float32
    )
    _, norm_back = jax.vjp(input_norm, inputs, norm_gain)
    grad_inputs, grad_norm_gain = norm_back(grad_normed)
    vector = repack(
        grad_norm_gain, grad_gate_gain, grad_kernel, grad_cbias, grad_bias, grad_rate, grad_skip
    )
    dp_count = lax.axis_size("dp")
    seq_count = lax.axis_size("seq")
    owner_rows = in_weight.shape[0]
    seq_place = lax.axis_index("seq")

    def select_rows(matrix):
        count = matrix.shape[0]
        grouped = matrix.reshape(count, dp_count, seq_count, owner_rows)
        chosen = lax.dynamic_slice_in_dim(grouped, seq_place, 1, 2)
        return chosen.reshape(count, dp_count * owner_rows)

    normed_piece = lax.all_gather(normed, "seq", axis=0, tiled=True)
    proj_piece = lax.all_gather(grad_proj, "seq", axis=0, tiled=True)
    upstream_piece = lax.all_gather(upstream, "seq", axis=0, tiled=True)
    out_piece = lax.all_gather(normed_out, "seq", axis=0, tiled=True)
    first = lax.dot_general(
        select_rows(normed_piece),
        proj_piece,
        (((0,), (0,)), ((), ())),
        preferred_element_type=jnp.float32,
    )
    second = lax.dot_general(
        select_rows(upstream_piece),
        out_piece,
        (((0,), (0,)), ((), ())),
        preferred_element_type=jnp.float32,
    )
    in_part, out_part = (
        lax.psum_scatter(
            first.reshape(dp_count, owner_rows, grad_proj.shape[1]).astype(jnp.bfloat16),
            "dp",
            scatter_dimension=0,
            tiled=True,
        ).astype(jnp.float32),
        lax.psum_scatter(
            second.reshape(dp_count, owner_rows, normed_out.shape[1]).astype(jnp.bfloat16),
            "dp",
            scatter_dimension=0,
            tiled=True,
        ).astype(jnp.float32),
    )
    in_grad = in_part.reshape(owner_rows, grad_proj.shape[1])
    out_grad = out_part.reshape(owner_rows, normed_out.shape[1])
    vec_grad = lax.psum(vector, ("dp", "seq"))
    in_new, in_m_new, in_v_new = adamw_update(in_weight, in_grad, in_m, in_v)
    out_new, out_m_new, out_v_new = adamw_update(out_weight, out_grad, out_m, out_v)
    vec_new, vec_m_new, vec_v_new = adamw_update(vec_params, vec_grad, vec_m, vec_v)
    return (
        outputs[None],
        (upstream_f + grad_inputs)[None],
        in_grad,
        out_grad,
        vec_grad,
        in_new,
        out_new,
        vec_new,
        in_m_new,
        in_v_new,
        out_m_new,
        out_v_new,
        vec_m_new,
        vec_v_new,
    )


def solution(mesh):
    in_specs = (
        P("dp", "seq", None),
        P("dp", "seq", None),
        P("dp", None),
        P(("dp", "seq"), None),
        P(("dp", "seq"), None),
        P(("dp", "seq"), None),
        P(("dp", "seq"), None),
        P(("dp", "seq"), None),
        P(("dp", "seq"), None),
        P(),
        P(),
        P(),
    )
    out_specs = (
        P("dp", "seq", None),
        P("dp", "seq", None),
        P(("dp", "seq"), None),
        P(("dp", "seq"), None),
        P(),
        P(("dp", "seq"), None),
        P(("dp", "seq"), None),
        P(),
        P(("dp", "seq"), None),
        P(("dp", "seq"), None),
        P(("dp", "seq"), None),
        P(("dp", "seq"), None),
        P(),
        P(),
    )
    return jax.shard_map(body, mesh=mesh, in_specs=in_specs, out_specs=out_specs, check_vma=False)
```

profile of v0, /device:TPU:0, one launch (start us, length us, event | category | flops | bytes accessed | tf_op | source)
XLA Modules:
  0.0 678.0 jit_solution(5091734478298455227)
XLA Ops:
  17.9 76.6 %all-gather.7.cloned.1.call-done = bf16[1024,4384]{1,0:T(8,128)(2,1)} async-done(((bf16[32,4384]{1,0:T(8,128)(2,1)}), bf16[1024,4384]{1,0:T(8,128)(2,1)}) %all-gather.7.cloned.1.call-update) | async-done | bytes 8978448 | tf_op jit(solution)/shard_map/all_gather | solution.py:153
  94.5 5.1 fusion.124
  128.1 152.6 %while.7 = (s32[]{:T(128)}, f32[32,64,128]{2,1,0:T(8,128)S(1)}, f32[1,32]{1,0:T(1,128)S(1)}, f32[32,64,128]{2,1,0:T(8,128)}, s32[]{:T(128)}) while((s32[]{:T(128)}, f32[32,64,128]{2,1,0:T(8,128)S(1)}, f32[1,32]{1,0:T(1,128)S(1)}, f32[32,64,128]{2,1,0:T(8,128)}, s32[]{:T(128)}) %tuple.149), condition=%wide.region_3.4_spmd, body=%wide.region_2.3_spmd.sunk | while | flops 524290 | bytes 7340261 | solution.py:196
  138.4 23.1 %collective-permute-start = (f32[32,64,128]{2,1,0:T(8,128)}, f32[32,64,128]{2,1,0:T(8,128)S(1)}, u32[]{:S(2)}, u32[]{:S(2)}) collective-permute-start(f32[32,64,128]{2,1,0:T(8,128)} %multiply_add_fusion.13), channel_id=1, source_target_pairs={{0,1},{1,2},{2,3},{3,4},{4,5},{5,6},{6,7},{8,9},{9,10},{10,11},{11... | collective-permute-start | bytes 3145736 | tf_op jit(solution)/shard_map/while/body/eval_jaxpr/ppermute | solution.py:27
  166.3 27.7 %collective-permute-start = (f32[32,64,128]{2,1,0:T(8,128)}, f32[32,64,128]{2,1,0:T(8,128)S(1)}, u32[]{:S(2)}, u32[]{:S(2)}) collective-permute-start(f32[32,64,128]{2,1,0:T(8,128)} %multiply_add_fusion.13), channel_id=1, source_target_pairs={{0,1},{1,2},{2,3},{3,4},{4,5},{5,6},{6,7},{8,9},{9,10},{10,11},{11... | collective-permute-start | bytes 3145736 | tf_op jit(solution)/shard_map/while/body/eval_jaxpr/ppermute | solution.py:27
  198.8 22.8 %collective-permute-start = (f32[32,64,128]{2,1,0:T(8,128)}, f32[32,64,128]{2,1,0:T(8,128)S(1)}, u32[]{:S(2)}, u32[]{:S(2)}) collective-permute-start(f32[32,64,128]{2,1,0:T(8,128)} %multiply_add_fusion.13), channel_id=1, source_target_pairs={{0,1},{1,2},{2,3},{3,4},{4,5},{5,6},{6,7},{8,9},{9,10},{10,11},{11... | collective-permute-start | bytes 3145736 | tf_op jit(solution)/shard_map/while/body/eval_jaxpr/ppermute | solution.py:27
  226.4 14.3 %collective-permute-start = (f32[32,64,128]{2,1,0:T(8,128)}, f32[32,64,128]{2,1,0:T(8,128)S(1)}, u32[]{:S(2)}, u32[]{:S(2)}) collective-permute-start(f32[32,64,128]{2,1,0:T(8,128)} %multiply_add_fusion.13), channel_id=1, source_target_pairs={{0,1},{1,2},{2,3},{3,4},{4,5},{5,6},{6,7},{8,9},{9,10},{10,11},{11... | collective-permute-start | bytes 3145736 | tf_op jit(solution)/shard_map/while/body/eval_jaxpr/ppermute | solution.py:27
  245.6 13.9 %collective-permute-start = (f32[32,64,128]{2,1,0:T(8,128)}, f32[32,64,128]{2,1,0:T(8,128)S(1)}, u32[]{:S(2)}, u32[]{:S(2)}) collective-permute-start(f32[32,64,128]{2,1,0:T(8,128)} %multiply_add_fusion.13), channel_id=1, source_target_pairs={{0,1},{1,2},{2,3},{3,4},{4,5},{5,6},{6,7},{8,9},{9,10},{10,11},{11... | collective-permute-start | bytes 3145736 | tf_op jit(solution)/shard_map/while/body/eval_jaxpr/ppermute | solution.py:27
  264.3 13.9 %collective-permute-start = (f32[32,64,128]{2,1,0:T(8,128)}, f32[32,64,128]{2,1,0:T(8,128)S(1)}, u32[]{:S(2)}, u32[]{:S(2)}) collective-permute-start(f32[32,64,128]{2,1,0:T(8,128)} %multiply_add_fusion.13), channel_id=1, source_target_pairs={{0,1},{1,2},{2,3},{3,4},{4,5},{5,6},{6,7},{8,9},{9,10},{10,11},{11... | collective-permute-start | bytes 3145736 | tf_op jit(solution)/shard_map/while/body/eval_jaxpr/ppermute | solution.py:27
  288.3 3.5 fusion.25
  294.3 3.4 multiply_reduce_fusion.13
  297.8 4.3 multiply_reduce_fusion.7
  302.2 4.2 multiply_reduce_fusion.6
  308.9 5.2 fusion.35
  323.6 134.3 %while.16 = (s32[]{:T(128)}, f32[32,64,128]{2,1,0:T(8,128)S(1)}, f32[1,32]{1,0:T(1,128)S(1)}, f32[32,64,128]{2,1,0:T(8,128)}, s32[]{:T(128)}, /*index=5*/s32[]{:T(128)}) while((s32[]{:T(128)}, f32[32,64,128]{2,1,0:T(8,128)S(1)}, f32[1,32]{1,0:T(1,128)S(1)}, f32[32,64,128]{2,1,0:T(8,128)}, s32[]{:T(128)}, ...), condition=%wide.region_8.9_spmd.clone, body=%wide.region_7.8_spmd.clone.sunk | while | flops 1310723 | bytes 6291703 | solution.py:222
  327.1 14.3 %collective-permute-done.1 = bf16[32,64,128]{2,1,0:T(8,128)(2,1)} collective-permute-done((bf16[32,64,128]{2,1,0:T(8,128)(2,1)}, bf16[32,64,128]{2,1,0:T(8,128)(2,1)}, u32[]{:S(2)}, u32[]{:S(2)}) %collective-permute-start.1) | collective-permute-done | bytes 524320 | tf_op jit(solution)/shard_map/while/body/eval_jaxpr/ppermute | solution.py:27
  346.0 10.2 %collective-permute-done.1 = bf16[32,64,128]{2,1,0:T(8,128)(2,1)} collective-permute-done((bf16[32,64,128]{2,1,0:T(8,128)(2,1)}, bf16[32,64,128]{2,1,0:T(8,128)(2,1)}, u32[]{:S(2)}, u32[]{:S(2)}) %collective-permute-start.1) | collective-permute-done | bytes 524320 | tf_op jit(solution)/shard_map/while/body/eval_jaxpr/ppermute | solution.py:27
  360.9 39.0 %collective-permute-done.1 = bf16[32,64,128]{2,1,0:T(8,128)(2,1)} collective-permute-done((bf16[32,64,128]{2,1,0:T(8,128)(2,1)}, bf16[32,64,128]{2,1,0:T(8,128)(2,1)}, u32[]{:S(2)}, u32[]{:S(2)}) %collective-permute-start.1) | collective-permute-done | bytes 524320 | tf_op jit(solution)/shard_map/while/body/eval_jaxpr/ppermute | solution.py:27
  404.5 9.5 %collective-permute-done.1 = bf16[32,64,128]{2,1,0:T(8,128)(2,1)} collective-permute-done((bf16[32,64,128]{2,1,0:T(8,128)(2,1)}, bf16[32,64,128]{2,1,0:T(8,128)(2,1)}, u32[]{:S(2)}, u32[]{:S(2)}) %collective-permute-start.1) | collective-permute-done | bytes 524320 | tf_op jit(solution)/shard_map/while/body/eval_jaxpr/ppermute | solution.py:27
  418.7 9.5 %collective-permute-done.1 = bf16[32,64,128]{2,1,0:T(8,128)(2,1)} collective-permute-done((bf16[32,64,128]{2,1,0:T(8,128)(2,1)}, bf16[32,64,128]{2,1,0:T(8,128)(2,1)}, u32[]{:S(2)}, u32[]{:S(2)}) %collective-permute-start.1) | collective-permute-done | bytes 524320 | tf_op jit(solution)/shard_map/while/body/eval_jaxpr/ppermute | solution.py:27
  432.8 9.5 %collective-permute-done.1 = bf16[32,64,128]{2,1,0:T(8,128)(2,1)} collective-permute-done((bf16[32,64,128]{2,1,0:T(8,128)(2,1)}, bf16[32,64,128]{2,1,0:T(8,128)(2,1)}, u32[]{:S(2)}, u32[]{:S(2)}) %collective-permute-start.1) | collective-permute-done | bytes 524320 | tf_op jit(solution)/shard_map/while/body/eval_jaxpr/ppermute | solution.py:27
  447.0 9.5 %collective-permute-done.1 = bf16[32,64,128]{2,1,0:T(8,128)(2,1)} collective-permute-done((bf16[32,64,128]{2,1,0:T(8,128)(2,1)}, bf16[32,64,128]{2,1,0:T(8,128)(2,1)}, u32[]{:S(2)}, u32[]{:S(2)}) %collective-permute-start.1) | collective-permute-done | bytes 524320 | tf_op jit(solution)/shard_map/while/body/eval_jaxpr/ppermute | solution.py:27
  476.2 5.1 fusion.28
  486.4 3.5 fusion.120
  505.8 7.9 %collective-permute-done.3 = f32[3,2304]{1,0:T(4,128)S(1)} collective-permute-done((f32[3,2304]{1,0:T(4,128)S(1)}, f32[3,2304]{1,0:T(4,128)S(1)}, u32[]{:S(2)}, u32[]{:S(2)}) %collective-permute-start.3) | collective-permute-done | bytes 27680 | tf_op jit(solution)/shard_map/ppermute | solution.py:27
  517.9 3.9 copy.220
  522.0 3.9 fusion.9
  526.2 4.7 fusion.31
  530.9 78.9 %all-gather.13.cloned.1.call-done = bf16[1024,4384]{1,0:T(8,128)(2,1)} async-done(((bf16[128,4384]{1,0:T(8,128)(2,1)}), bf16[1024,4384]{1,0:T(8,128)(2,1)}) %all-gather.13.cloned.1.call-update) | async-done | bytes 8978448 | tf_op jit(solution)/shard_map/all_gather | solution.py:269
  609.9 6.0 fusion.4
  617.2 7.0 %multiply_reduce_fusion.14 = (f32[1024]{0:T(1024)S(1)}, f32[128]{0:T(128)S(1)}, f32[128,1024]{1,0:T(8,128)S(1)}) fusion(f32[1,128,1024]{2,1,0:T(8,128)S(1)} %copy-done.2, f32[128]{0:T(128)S(1)} %copy-done.78, f32[1024]{0:T(1024)S(1)} %slice.169, bf16[128,4384]{1,0:T(8,128)(2,1)S(1)} %copy-done.3, bf16[1024,4384]{1,0:T(8,128)(2,1)} %all-gather.7.cloned.1.call-done), kind=kOutput, calls=%fused_computation.102 | convolution fusion | flops 1150024576 | bytes 11158528 | tf_op jit(solution)/shard_map/dot_general | solution.py:249
  624.3 39.2 %psum.7 = f32[14688]{0:T(1024)S(1)} all-reduce(f32[14688]{0:T(1024)S(1)} %concatenate.23), channel_id=1, replica_groups=mesh['dp'=4,'seq'=8] {'dp','seq'}, use_global_device_ids=true, to_apply=%region_33.34 | all-reduce | flops 14688 | bytes 117504 | tf_op jit(solution)/shard_map/psum | solution.py:300
  (325 shorter events, 182.0 us)
Async XLA Ops:
  7.2 87.3 %all-gather.7.cloned.1.call-start = ((), (), s32[]{:S(2)}) async-start(), calls=%async_computation.2 | async-start | bytes 9461760 | tf_op jit(solution)/shard_map/all_gather | solution.py:153
  9.1 288.6 %all-gather.9.cloned.1.call-start = ((), (), s32[]{:S(2)}) async-start(), calls=%async_computation.3 | async-start | bytes 4325376 | tf_op jit(solution)/shard_map/all_gather | solution.py:154
  9.9 505.0 %all-gather.11.cloned.1.call-start = ((), (), s32[]{:S(2)}) async-start(), calls=%async_computation.4 | async-start | bytes 2359296 | tf_op jit(solution)/shard_map/all_gather | solution.py:268
  11.0 506.9 %all-gather.15.cloned.1.call-start = ((), (), s32[]{:S(2)}) async-start(), calls=%async_computation.6 | async-start | bytes 2359296 | tf_op jit(solution)/shard_map/all_gather | solution.py:270
  11.8 510.1 %all-gather.17.cloned.1.call-start = ((), (), s32[]{:S(2)}) async-start(), calls=%async_computation.7 | async-start | bytes 4718592 | tf_op jit(solution)/shard_map/all_gather | solution.py:271
  13.3 90.8 %copy-start.76 = (f32[32]{0:T(128)}, f32[32]{0:T(128)S(1)}, u32[]{:S(2)}) copy-start(f32[32]{0:T(128)S(1)} %get-tuple-element.499) | copy-start | bytes 388
  13.3 91.0 %copy-start.59 = (f32[32]{0:T(128)}, f32[32]{0:T(128)S(1)}, u32[]{:S(2)}) copy-start(f32[32]{0:T(128)S(1)} %get-tuple-element.498) | copy-start | bytes 388
  17.9 101.3 %copy-start.65 = (f32[128]{0:T(128)}, f32[128]{0:T(128)S(1)}, u32[]{:S(2)}) copy-start(f32[128]{0:T(128)S(1)} %get-tuple-element.509) | copy-start | bytes 1540
  99.6 16.0 %copy-start.6 = (f32[128,4384]{1,0:T(8,128)}, f32[128,4384]{1,0:T(8,128)S(1)}, u32[]{:S(2)}) copy-start(f32[128,4384]{1,0:T(8,128)S(1)} %get-tuple-element.518) | copy-start | bytes 6733828
  101.3 16.9 %collective-permute-start.2 = (bf16[3,2304]{1,0:T(4,128)(2,1)}, bf16[3,2304]{1,0:T(4,128)(2,1)}, u32[]{:S(2)}, u32[]{:S(2)}) collective-permute-start(bf16[3,2304]{1,0:T(4,128)(2,1)} %slice.205), channel_id=1, source_target_pairs={{0,1},{1,2},{2,3},{3,4},{4,5},{5,6},{6,7},{8,9},{9,10},{10,11},{11... | collective-permute-start | bytes 41480 | tf_op jit(solution)/shard_map/ppermute | solution.py:27
  108.6 212.0 %copy-start.27 = (f32[128,32]{0,1:T(8,128)}, f32[128,32]{0,1:T(8,128)S(1)}, u32[]{:S(2)}) copy-start(f32[128,32]{0,1:T(8,128)S(1)} %copy.204) | copy-start | bytes 49156
  130.9 5.0 collective-permute-start
  138.4 25.5 %collective-permute-start = (f32[32,64,128]{2,1,0:T(8,128)}, f32[32,64,128]{2,1,0:T(8,128)S(1)}, u32[]{:S(2)}, u32[]{:S(2)}) collective-permute-start(f32[32,64,128]{2,1,0:T(8,128)} %multiply_add_fusion.13), channel_id=1, source_target_pairs={{0,1},{1,2},{2,3},{3,4},{4,5},{5,6},{6,7},{8,9},{9,10},{10,11},{11... | collective-permute-start | bytes 3145736 | tf_op jit(solution)/shard_map/while/body/eval_jaxpr/ppermute | solution.py:27
  166.3 30.1 %collective-permute-start = (f32[32,64,128]{2,1,0:T(8,128)}, f32[32,64,128]{2,1,0:T(8,128)S(1)}, u32[]{:S(2)}, u32[]{:S(2)}) collective-permute-start(f32[32,64,128]{2,1,0:T(8,128)} %multiply_add_fusion.13), channel_id=1, source_target_pairs={{0,1},{1,2},{2,3},{3,4},{4,5},{5,6},{6,7},{8,9},{9,10},{10,11},{11... | collective-permute-start | bytes 3145736 | tf_op jit(solution)/shard_map/while/body/eval_jaxpr/ppermute | solution.py:27
  198.8 25.3 %collective-permute-start = (f32[32,64,128]{2,1,0:T(8,128)}, f32[32,64,128]{2,1,0:T(8,128)S(1)}, u32[]{:S(2)}, u32[]{:S(2)}) collective-permute-start(f32[32,64,128]{2,1,0:T(8,128)} %multiply_add_fusion.13), channel_id=1, source_target_pairs={{0,1},{1,2},{2,3},{3,4},{4,5},{5,6},{6,7},{8,9},{9,10},{10,11},{11... | collective-permute-start | bytes 3145736 | tf_op jit(solution)/shard_map/while/body/eval_jaxpr/ppermute | solution.py:27
  226.4 16.7 %collective-permute-start = (f32[32,64,128]{2,1,0:T(8,128)}, f32[32,64,128]{2,1,0:T(8,128)S(1)}, u32[]{:S(2)}, u32[]{:S(2)}) collective-permute-start(f32[32,64,128]{2,1,0:T(8,128)} %multiply_add_fusion.13), channel_id=1, source_target_pairs={{0,1},{1,2},{2,3},{3,4},{4,5},{5,6},{6,7},{8,9},{9,10},{10,11},{11... | collective-permute-start | bytes 3145736 | tf_op jit(solution)/shard_map/while/body/eval_jaxpr/ppermute | solution.py:27
  245.6 16.3 %collective-permute-start = (f32[32,64,128]{2,1,0:T(8,128)}, f32[32,64,128]{2,1,0:T(8,128)S(1)}, u32[]{:S(2)}, u32[]{:S(2)}) collective-permute-start(f32[32,64,128]{2,1,0:T(8,128)} %multiply_add_fusion.13), channel_id=1, source_target_pairs={{0,1},{1,2},{2,3},{3,4},{4,5},{5,6},{6,7},{8,9},{9,10},{10,11},{11... | collective-permute-start | bytes 3145736 | tf_op jit(solution)/shard_map/while/body/eval_jaxpr/ppermute | solution.py:27
  264.3 16.3 %collective-permute-start = (f32[32,64,128]{2,1,0:T(8,128)}, f32[32,64,128]{2,1,0:T(8,128)S(1)}, u32[]{:S(2)}, u32[]{:S(2)}) collective-permute-start(f32[32,64,128]{2,1,0:T(8,128)} %multiply_add_fusion.13), channel_id=1, source_target_pairs={{0,1},{1,2},{2,3},{3,4},{4,5},{5,6},{6,7},{8,9},{9,10},{10,11},{11... | collective-permute-start | bytes 3145736 | tf_op jit(solution)/shard_map/while/body/eval_jaxpr/ppermute | solution.py:27
  323.5 286.4 %all-gather.13.cloned.1.call-start = ((), (), s32[]{:S(2)}) async-start(), calls=%async_computation.5 | async-start | bytes 10321920 | tf_op jit(solution)/shard_map/all_gather | solution.py:269
  325.8 15.6 %collective-permute-start.1 = (bf16[32,64,128]{2,1,0:T(8,128)(2,1)}, bf16[32,64,128]{2,1,0:T(8,128)(2,1)}, u32[]{:S(2)}, u32[]{:S(2)}) collective-permute-start(bf16[32,64,128]{2,1,0:T(8,128)(2,1)} %fusion.145), channel_id=1, source_target_pairs={{1,0},{2,1},{3,2},{4,3},{5,4},{6,5},{7,6},{9,8},{10,9},{11,10},{12... | collective-permute-start | bytes 1572872 | tf_op jit(solution)/shard_map/while/body/eval_jaxpr/ppermute | solution.py:27
  344.7 11.4 %collective-permute-start.1 = (bf16[32,64,128]{2,1,0:T(8,128)(2,1)}, bf16[32,64,128]{2,1,0:T(8,128)(2,1)}, u32[]{:S(2)}, u32[]{:S(2)}) collective-permute-start(bf16[32,64,128]{2,1,0:T(8,128)(2,1)} %fusion.145), channel_id=1, source_target_pairs={{1,0},{2,1},{3,2},{4,3},{5,4},{6,5},{7,6},{9,8},{10,9},{11,10},{12... | collective-permute-start | bytes 1572872 | tf_op jit(solution)/shard_map/while/body/eval_jaxpr/ppermute | solution.py:27
  359.6 40.2 %collective-permute-start.1 = (bf16[32,64,128]{2,1,0:T(8,128)(2,1)}, bf16[32,64,128]{2,1,0:T(8,128)(2,1)}, u32[]{:S(2)}, u32[]{:S(2)}) collective-permute-start(bf16[32,64,128]{2,1,0:T(8,128)(2,1)} %fusion.145), channel_id=1, source_target_pairs={{1,0},{2,1},{3,2},{4,3},{5,4},{6,5},{7,6},{9,8},{10,9},{11,10},{12... | collective-permute-start | bytes 1572872 | tf_op jit(solution)/shard_map/while/body/eval_jaxpr/ppermute | solution.py:27
  403.2 10.8 %collective-permute-start.1 = (bf16[32,64,128]{2,1,0:T(8,128)(2,1)}, bf16[32,64,128]{2,1,0:T(8,128)(2,1)}, u32[]{:S(2)}, u32[]{:S(2)}) collective-permute-start(bf16[32,64,128]{2,1,0:T(8,128)(2,1)} %fusion.145), channel_id=1, source_target_pairs={{1,0},{2,1},{3,2},{4,3},{5,4},{6,5},{7,6},{9,8},{10,9},{11,10},{12... | collective-permute-start | bytes 1572872 | tf_op jit(solution)/shard_map/while/body/eval_jaxpr/ppermute | solution.py:27
  417.4 10.8 %collective-permute-start.1 = (bf16[32,64,128]{2,1,0:T(8,128)(2,1)}, bf16[32,64,128]{2,1,0:T(8,128)(2,1)}, u32[]{:S(2)}, u32[]{:S(2)}) collective-permute-start(bf16[32,64,128]{2,1,0:T(8,128)(2,1)} %fusion.145), channel_id=1, source_target_pairs={{1,0},{2,1},{3,2},{4,3},{5,4},{6,5},{7,6},{9,8},{10,9},{11,10},{12... | collective-permute-start | bytes 1572872 | tf_op jit(solution)/shard_map/while/body/eval_jaxpr/ppermute | solution.py:27
  431.6 10.8 %collective-permute-start.1 = (bf16[32,64,128]{2,1,0:T(8,128)(2,1)}, bf16[32,64,128]{2,1,0:T(8,128)(2,1)}, u32[]{:S(2)}, u32[]{:S(2)}) collective-permute-start(bf16[32,64,128]{2,1,0:T(8,128)(2,1)} %fusion.145), channel_id=1, source_target_pairs={{1,0},{2,1},{3,2},{4,3},{5,4},{6,5},{7,6},{9,8},{10,9},{11,10},{12... | collective-permute-start | bytes 1572872 | tf_op jit(solution)/shard_map/while/body/eval_jaxpr/ppermute | solution.py:27
  445.7 10.8 %collective-permute-start.1 = (bf16[32,64,128]{2,1,0:T(8,128)(2,1)}, bf16[32,64,128]{2,1,0:T(8,128)(2,1)}, u32[]{:S(2)}, u32[]{:S(2)}) collective-permute-start(bf16[32,64,128]{2,1,0:T(8,128)(2,1)} %fusion.145), channel_id=1, source_target_pairs={{1,0},{2,1},{3,2},{4,3},{5,4},{6,5},{7,6},{9,8},{10,9},{11,10},{12... | collective-permute-start | bytes 1572872 | tf_op jit(solution)/shard_map/while/body/eval_jaxpr/ppermute | solution.py:27
  503.9 9.8 %collective-permute-start.3 = (f32[3,2304]{1,0:T(4,128)S(1)}, f32[3,2304]{1,0:T(4,128)S(1)}, u32[]{:S(2)}, u32[]{:S(2)}) collective-permute-start(f32[3,2304]{1,0:T(4,128)S(1)} %pad_add_fusion.1), channel_id=1, source_target_pairs={{1,0},{2,1},{3,2},{4,3},{5,4},{6,5},{7,6},{9,8},{10,9},{11,10},{12... | collective-permute-start | bytes 82952 | tf_op jit(solution)/shard_map/ppermute | solution.py:27
  505.7 8.0 %copy-start.19 = (bf16[128,2048]{1,0:T(8,128)(2,1)S(1)}, bf16[128,2048]{1,0:T(8,128)(2,1)}, u32[]{:S(2)}) copy-start(bf16[128,2048]{1,0:T(8,128)(2,1)} %get-tuple-element.479) | copy-start | bytes 1572868
  514.9 151.3 %reduce-scatter.9.cloned.1.call-start = ((), (), s32[]{:S(2)}) async-start(), calls=%async_computation.9 | async-start | bytes 655360
  525.9 142.6 %reduce-scatter.7.cloned.1.call-start = ((), (), s32[]{:S(2)}) async-start(), calls=%async_computation.8 | async-start | bytes 1433600
  617.2 46.3 %copy-start.82 = (f32[128]{0:T(128)S(1)}, f32[128]{0:T(128)}, u32[]{:S(2)}) copy-start(f32[128]{0:T(128)} %copy-done.81) | copy-start | bytes 1540
  617.2 46.3 %copy-start.21 = (f32[1,128,1024]{2,1,0:T(8,128)S(1)}, f32[1,128,1024]{2,1,0:T(8,128)}, u32[]{:S(2)}) copy-start(f32[1,128,1024]{2,1,0:T(8,128)} %param.17) | copy-start | bytes 1572868
  (76 other events, 240.5 us)
Sparse Core Ops, SparseCore 0:
  11.4 82.9 all-gather.6
  98.1 60.2 all-gather.8
  160.5 32.0 all-gather.10
  194.6 31.4 all-gather.14
  323.6 73.2 all-gather.16
  515.0 94.8 all-gather.12
  613.3 23.5 reduce-scatter.8
  639.7 28.6 reduce-scatter.6
where the time goes:
time: 686 us; the launch traced here: 678 us
  waiting for transfers between devices  282 us (41%)
  starting transfers between devices  132 us (19%)
  other arithmetic  89.3 us (13%)
  matrix products  67.5 us (10%)
  local copies, waits for them, and re-layouts  51.8 us (8%)
  blocking collectives  39.2 us (6%)
  between operations  15.4 us (2%)
    ppermute x16, starting transfers between devices, shifted_2(): return lax.ppermute(block, axis, route)  131 us
    ppermute x16, waiting for transfers between devices, shifted_2(): return lax.ppermute(block, axis, route)  126 us
    all_gather x1, waiting for transfers between devices, body(): proj_piece = lax.all_gather(grad_proj, 'seq', axis=0, tiled=True)  78.9 us
    all_gather x1, waiting for transfers between devices, body(): lax.all_gather(in_weight.astype(jnp.bfloat16), ('dp', 'seq'), axis=0, til...  76.6 us
    psum x1, blocking collectives, body(): vec_grad = lax.psum(vector, ('dp', 'seq'))  39.2 us
    add x7, other arithmetic, relay(): return shifted_2(decay[:, None, None] * entry_now + local_state, 'seq', 1)  16.8 us
    convert_element_type x7, other arithmetic, back_relay(): (own_part + decay[:, None, None] * later).astype(jnp.bfloat16)  15.5 us
    dot_general x3, matrix products, ssd_block(): inside = jnp.einsum('hij,jhp->ihp', mixing, values, precision=top_precision)  13.7 us
  transfers between devices with their start and end apart: 24, of which 18 were waited for; matrix products, arithmetic and copies ran while one was open for 30% of the time, Pallas kernels for 0%

commit v1 on v0

--- a/solution.py
+++ b/solution.py
@@ -19,6 +19,31 @@
 decay_rate = 0.1
 adam_eps = 1e-08
 top_precision = lax.Precision.HIGHEST
+
+
+def work_lanes(local):
+    by_rank = []
+    b_next, plain, v_next = (lax.axis_size("seq"), lax.axis_index("seq"), local.shape[0])
+    for ix in [*range(b_next)]:
+        by_rank.append((ix, (ix + 1) % b_next))
+    seen = []
+    for ix in tuple(range(b_next)):
+        seen.append((ix, (ix - 1) % b_next))
+    field_out = jnp.zeros((*local.shape[:0], b_next * v_next, *local.shape[1:]), local.dtype)
+    field_out = lax.dynamic_update_slice_in_dim(field_out, local, plain * v_next, axis=0)
+    item_now = block_out = local
+    f_next = b_next // 2
+    for ii in tuple(range(1, f_next + 1)):
+        item_now = lax.ppermute(item_now, axis_name="seq", perm=by_rank)
+        field_out = lax.dynamic_update_slice_in_dim(
+            field_out, item_now, (plain - ii) % b_next * v_next, axis=0
+        )
+        if ii < b_next - f_next:
+            block_out = lax.ppermute(block_out, axis_name="seq", perm=seen)
+            field_out = lax.dynamic_update_slice_in_dim(
+                field_out, block_out, (plain + ii) % b_next * v_next, axis=0
+            )
+    return field_out
 
 
 def shifted_2(block, axis, distance):
@@ -266,7 +291,7 @@
         return chosen.reshape(count, dp_count * owner_rows)
 
     normed_piece = lax.all_gather(normed, "seq", axis=0, tiled=True)
-    proj_piece = lax.all_gather(grad_proj, "seq", axis=0, tiled=True)
+    proj_piece = work_lanes(grad_proj)
     upstream_piece = lax.all_gather(upstream, "seq", axis=0, tiled=True)
     out_piece = lax.all_gather(normed_out, "seq", axis=0, tiled=True)
     first = lax.dot_general(

time: 686 us -> 729 us (1.063)
  starting transfers between devices: 132 us -> 166 us
  blocking collectives: 39.2 us -> 47.5 us
  local copies, waits for them, and re-layouts: 51.8 us -> 59.7 us
    ppermute x0 -> x7, waiting for transfers between devices: none -> 79.4 us  [the longest x4 68.3 us: work_lanes(): item_now = lax.ppermute(item_now, axis_name='seq', perm=by_rank)]
    all_gather x1 -> x0, waiting for transfers between devices: 78.9 us -> none  [body(): proj_piece = lax.all_gather(grad_proj, 'seq', axis=0, tiled=True)]
    ppermute x16, waiting for transfers between devices: 126 us -> 95.8 us  [shifted_2(): return lax.ppermute(block, axis, route)]
    ppermute x0 -> x7, starting transfers between devices: none -> 25.2 us  [the longest x4 15.9 us: work_lanes(): item_now = lax.ppermute(item_now, axis_name='seq', perm=by_rank)]
    unnamed x10 -> x9, waiting for transfers between devices: 0.41 us -> 23.1 us
    ppermute x16, starting transfers between devices: 131 us -> 140 us  [shifted_2(): return lax.ppermute(block, axis, route)]
    psum x1, blocking collectives: 39.2 us -> 47.5 us  [body(): vec_grad = lax.psum(vector, ('dp', 'seq'))]
  transfers between devices with their start and end apart: 24 -> 30, of which waited for: 18 -> 24; matrix products, arithmetic and copies ran while one was open for 30% -> 29% of each run, Pallas kernels for 0% -> 0%
where the time goes in v1:
time: 729 us; the launch traced here: 721 us
  waiting for transfers between devices  275 us (38%)
  starting transfers between devices  166 us (23%)
  other arithmetic  91.2 us (13%)
  matrix products  65.1 us (9%)
  local copies, waits for them, and re-layouts  59.7 us (8%)
  blocking collectives  47.5 us (7%)
  between operations  15.5 us (2%)
    ppermute x16, starting transfers between devices, shifted_2(): return lax.ppermute(block, axis, route)  140 us
    ppermute x16, waiting for transfers between devices, shifted_2(): return lax.ppermute(block, axis, route)  95.8 us
    all_gather x1, waiting for transfers between devices, body(): lax.all_gather(in_weight.astype(jnp.bfloat16), ('dp', 'seq'), axis=0, til...  77.1 us
    ppermute x4, waiting for transfers between devices, work_lanes(): item_now = lax.ppermute(item_now, axis_name='seq', perm=by_rank)  68.3 us
    psum x1, blocking collectives, body(): vec_grad = lax.psum(vector, ('dp', 'seq'))  47.5 us
    unnamed x9, waiting for transfers between devices  23.1 us
    add x7, other arithmetic, relay(): return shifted_2(decay[:, None, None] * entry_now + local_state, 'seq', 1)  17.6 us
    ppermute x4, starting transfers between devices, work_lanes(): item_now = lax.ppermute(item_now, axis_name='seq', perm=by_rank)  15.9 us
  transfers between devices with their start and end apart: 30, of which 24 were waited for; matrix products, arithmetic and copies ran while one was open for 29% of the time, Pallas kernels for 0%

profile of v1, /device:TPU:0, one launch (start us, length us, event | category | flops | bytes accessed | tf_op | source)
XLA Modules:
  0.0 721.1 jit_solution(7520746127508885010)
XLA Ops:
  17.3 77.1 %all-gather.6.cloned.1.call-done = bf16[1024,4384]{1,0:T(8,128)(2,1)} async-done(((bf16[32,4384]{1,0:T(8,128)(2,1)}), bf16[1024,4384]{1,0:T(8,128)(2,1)}) %all-gather.6.cloned.1.call-update) | async-done | bytes 8978448 | tf_op jit(solution)/shard_map/all_gather | solution.py:178
  94.5 5.1 fusion.124
  130.9 162.2 %while.7 = (s32[]{:T(128)}, f32[32,64,128]{2,1,0:T(8,128)S(1)}, f32[1,32]{1,0:T(1,128)S(1)}, f32[32,64,128]{2,1,0:T(8,128)}, s32[]{:T(128)}) while((s32[]{:T(128)}, f32[32,64,128]{2,1,0:T(8,128)S(1)}, f32[1,32]{1,0:T(1,128)S(1)}, f32[32,64,128]{2,1,0:T(8,128)}, s32[]{:T(128)}) %tuple.147), condition=%wide.region_3.4_spmd, body=%wide.region_2.3_spmd.sunk | while | flops 524290 | bytes 7340261 | solution.py:221
  141.8 22.8 %collective-permute-start = (f32[32,64,128]{2,1,0:T(8,128)}, f32[32,64,128]{2,1,0:T(8,128)S(1)}, u32[]{:S(2)}, u32[]{:S(2)}) collective-permute-start(f32[32,64,128]{2,1,0:T(8,128)} %multiply_add_fusion.13), channel_id=1, source_target_pairs={{0,1},{1,2},{2,3},{3,4},{4,5},{5,6},{6,7},{8,9},{9,10},{10,11},{11... | collective-permute-start | bytes 3145736 | tf_op jit(solution)/shard_map/while/body/eval_jaxpr/ppermute | solution.py:52
  169.5 30.7 %collective-permute-start = (f32[32,64,128]{2,1,0:T(8,128)}, f32[32,64,128]{2,1,0:T(8,128)S(1)}, u32[]{:S(2)}, u32[]{:S(2)}) collective-permute-start(f32[32,64,128]{2,1,0:T(8,128)} %multiply_add_fusion.13), channel_id=1, source_target_pairs={{0,1},{1,2},{2,3},{3,4},{4,5},{5,6},{6,7},{8,9},{9,10},{10,11},{11... | collective-permute-start | bytes 3145736 | tf_op jit(solution)/shard_map/while/body/eval_jaxpr/ppermute | solution.py:52
  205.1 29.2 %collective-permute-start = (f32[32,64,128]{2,1,0:T(8,128)}, f32[32,64,128]{2,1,0:T(8,128)S(1)}, u32[]{:S(2)}, u32[]{:S(2)}) collective-permute-start(f32[32,64,128]{2,1,0:T(8,128)} %multiply_add_fusion.13), channel_id=1, source_target_pairs={{0,1},{1,2},{2,3},{3,4},{4,5},{5,6},{6,7},{8,9},{9,10},{10,11},{11... | collective-permute-start | bytes 3145736 | tf_op jit(solution)/shard_map/while/body/eval_jaxpr/ppermute | solution.py:52
  239.2 13.9 %collective-permute-start = (f32[32,64,128]{2,1,0:T(8,128)}, f32[32,64,128]{2,1,0:T(8,128)S(1)}, u32[]{:S(2)}, u32[]{:S(2)}) collective-permute-start(f32[32,64,128]{2,1,0:T(8,128)} %multiply_add_fusion.13), channel_id=1, source_target_pairs={{0,1},{1,2},{2,3},{3,4},{4,5},{5,6},{6,7},{8,9},{9,10},{10,11},{11... | collective-permute-start | bytes 3145736 | tf_op jit(solution)/shard_map/while/body/eval_jaxpr/ppermute | solution.py:52
  258.0 13.9 %collective-permute-start = (f32[32,64,128]{2,1,0:T(8,128)}, f32[32,64,128]{2,1,0:T(8,128)S(1)}, u32[]{:S(2)}, u32[]{:S(2)}) collective-permute-start(f32[32,64,128]{2,1,0:T(8,128)} %multiply_add_fusion.13), channel_id=1, source_target_pairs={{0,1},{1,2},{2,3},{3,4},{4,5},{5,6},{6,7},{8,9},{9,10},{10,11},{11... | collective-permute-start | bytes 3145736 | tf_op jit(solution)/shard_map/while/body/eval_jaxpr/ppermute | solution.py:52
  276.8 13.9 %collective-permute-start = (f32[32,64,128]{2,1,0:T(8,128)}, f32[32,64,128]{2,1,0:T(8,128)S(1)}, u32[]{:S(2)}, u32[]{:S(2)}) collective-permute-start(f32[32,64,128]{2,1,0:T(8,128)} %multiply_add_fusion.13), channel_id=1, source_target_pairs={{0,1},{1,2},{2,3},{3,4},{4,5},{5,6},{6,7},{8,9},{9,10},{10,11},{11... | collective-permute-start | bytes 3145736 | tf_op jit(solution)/shard_map/while/body/eval_jaxpr/ppermute | solution.py:52
  298.5 4.9 fusion.25
  323.4 104.7 %while.16 = (s32[]{:T(128)}, f32[32,64,128]{2,1,0:T(8,128)S(1)}, f32[1,32]{1,0:T(1,128)S(1)}, f32[32,64,128]{2,1,0:T(8,128)}, s32[]{:T(128)}, /*index=5*/s32[]{:T(128)}) while((s32[]{:T(128)}, f32[32,64,128]{2,1,0:T(8,128)S(1)}, f32[1,32]{1,0:T(1,128)S(1)}, f32[32,64,128]{2,1,0:T(8,128)}, s32[]{:T(128)}, ...), condition=%wide.region_8.9_spmd.clone, body=%wide.region_7.8_spmd.clone.sunk | while | flops 1310723 | bytes 6291703 | solution.py:247
  326.9 14.3 %collective-permute-done.1 = bf16[32,64,128]{2,1,0:T(8,128)(2,1)} collective-permute-done((bf16[32,64,128]{2,1,0:T(8,128)(2,1)}, bf16[32,64,128]{2,1,0:T(8,128)(2,1)}, u32[]{:S(2)}, u32[]{:S(2)}) %collective-permute-start.1) | collective-permute-done | bytes 524320 | tf_op jit(solution)/shard_map/while/body/eval_jaxpr/ppermute | solution.py:52
  345.9 10.2 %collective-permute-done.1 = bf16[32,64,128]{2,1,0:T(8,128)(2,1)} collective-permute-done((bf16[32,64,128]{2,1,0:T(8,128)(2,1)}, bf16[32,64,128]{2,1,0:T(8,128)(2,1)}, u32[]{:S(2)}, u32[]{:S(2)}) %collective-permute-start.1) | collective-permute-done | bytes 524320 | tf_op jit(solution)/shard_map/while/body/eval_jaxpr/ppermute | solution.py:52
  360.7 9.5 %collective-permute-done.1 = bf16[32,64,128]{2,1,0:T(8,128)(2,1)} collective-permute-done((bf16[32,64,128]{2,1,0:T(8,128)(2,1)}, bf16[32,64,128]{2,1,0:T(8,128)(2,1)}, u32[]{:S(2)}, u32[]{:S(2)}) %collective-permute-start.1) | collective-permute-done | bytes 524320 | tf_op jit(solution)/shard_map/while/body/eval_jaxpr/ppermute | solution.py:52
  374.9 9.5 %collective-permute-done.1 = bf16[32,64,128]{2,1,0:T(8,128)(2,1)} collective-permute-done((bf16[32,64,128]{2,1,0:T(8,128)(2,1)}, bf16[32,64,128]{2,1,0:T(8,128)(2,1)}, u32[]{:S(2)}, u32[]{:S(2)}) %collective-permute-start.1) | collective-permute-done | bytes 524320 | tf_op jit(solution)/shard_map/while/body/eval_jaxpr/ppermute | solution.py:52
  389.1 9.5 %collective-permute-done.1 = bf16[32,64,128]{2,1,0:T(8,128)(2,1)} collective-permute-done((bf16[32,64,128]{2,1,0:T(8,128)(2,1)}, bf16[32,64,128]{2,1,0:T(8,128)(2,1)}, u32[]{:S(2)}, u32[]{:S(2)}) %collective-permute-start.1) | collective-permute-done | bytes 524320 | tf_op jit(solution)/shard_map/while/body/eval_jaxpr/ppermute | solution.py:52
  403.3 9.5 %collective-permute-done.1 = bf16[32,64,128]{2,1,0:T(8,128)(2,1)} collective-permute-done((bf16[32,64,128]{2,1,0:T(8,128)(2,1)}, bf16[32,64,128]{2,1,0:T(8,128)(2,1)}, u32[]{:S(2)}, u32[]{:S(2)}) %collective-permute-start.1) | collective-permute-done | bytes 524320 | tf_op jit(solution)/shard_map/while/body/eval_jaxpr/ppermute | solution.py:52
  417.4 9.5 %collective-permute-done.1 = bf16[32,64,128]{2,1,0:T(8,128)(2,1)} collective-permute-done((bf16[32,64,128]{2,1,0:T(8,128)(2,1)}, bf16[32,64,128]{2,1,0:T(8,128)(2,1)}, u32[]{:S(2)}, u32[]{:S(2)}) %collective-permute-start.1) | collective-permute-done | bytes 524320 | tf_op jit(solution)/shard_map/while/body/eval_jaxpr/ppermute | solution.py:52
  455.3 5.1 fusion.28
  487.2 6.9 collective-permute-done.3
  508.8 4.5 fusion.31
  514.9 24.6 %collective-permute-done.4 = bf16[128,4384]{0,1:T(8,128)(2,1)} collective-permute-done((bf16[128,4384]{0,1:T(8,128)(2,1)S(1)}, bf16[128,4384]{0,1:T(8,128)(2,1)}, u32[]{:S(2)}, u32[]{:S(2)}) %collective-permute-start.4) | collective-permute-done | bytes 1122336 | tf_op jit(solution)/shard_map/ppermute | solution.py:37
  544.0 4.6 collective-permute-done.5
  555.7 19.9 %collective-permute-done.6 = bf16[128,4384]{0,1:T(8,128)(2,1)S(1)} collective-permute-done((bf16[128,4384]{0,1:T(8,128)(2,1)}, bf16[128,4384]{0,1:T(8,128)(2,1)S(1)}, u32[]{:S(2)}, u32[]{:S(2)}) %collective-permute-start.6) | collective-permute-done | bytes 1122336 | tf_op jit(solution)/shard_map/ppermute | solution.py:37
  575.6 4.6 collective-permute-start.8
  586.6 12.4 %collective-permute-done.8 = bf16[128,4384]{0,1:T(8,128)(2,1)S(1)} collective-permute-done((bf16[128,4384]{0,1:T(8,128)(2,1)S(1)}, bf16[128,4384]{0,1:T(8,128)(2,1)S(1)}, u32[]{:S(2)}, u32[]{:S(2)}) %collective-permute-start.8) | collective-permute-done | bytes 1122336 | tf_op jit(solution)/shard_map/ppermute | solution.py:37
  603.5 4.5 collective-permute-done.9
  608.4 11.4 %collective-permute-done.10 = bf16[128,4384]{0,1:T(8,128)(2,1)S(1)} collective-permute-done((bf16[128,4384]{0,1:T(8,128)(2,1)S(1)}, bf16[128,4384]{0,1:T(8,128)(2,1)S(1)}, u32[]{:S(2)}, u32[]{:S(2)}) %collective-permute-start.10) | collective-permute-done | bytes 1122336 | tf_op jit(solution)/shard_map/ppermute | solution.py:37
  620.2 5.0 fusion.4
  626.3 6.8 multiply_reduce_fusion.14
  633.2 47.5 %psum.7 = f32[14688]{0:T(1024)S(1)} all-reduce(f32[14688]{0:T(1024)S(1)} %concatenate.23), channel_id=1, replica_groups=mesh['dp'=4,'seq'=8] {'dp','seq'}, use_global_device_ids=true, to_apply=%region_33.34 | all-reduce | flops 14688 | bytes 117504 | tf_op jit(solution)/shard_map/psum | solution.py:325
  689.1 23.0 %reduce-scatter.9.cloned.1.call-done = bf16[1,32,2048]{2,1,0:T(8,128)(2,1)} async-done(((bf16[4,32,2048]{2,1,0:T(8,128)(2,1)}), bf16[1,32,2048]{2,1,0:T(8,128)(2,1)}) %reduce-scatter.9.cloned.1.call-update) | async-done | bytes 131088
  (336 shorter events, 240.3 us)
Async XLA Ops:
  7.2 87.3 %all-gather.6.cloned.1.call-start = ((), (), s32[]{:S(2)}) async-start(), calls=%async_computation.2 | async-start | bytes 9461760 | tf_op jit(solution)/shard_map/all_gather | solution.py:178
  9.1 300.3 %all-gather.8.cloned.1.call-start = ((), (), s32[]{:S(2)}) async-start(), calls=%async_computation.3 | async-start | bytes 4325376 | tf_op jit(solution)/shard_map/all_gather | solution.py:179
  9.9 490.7 %all-gather.10.cloned.1.call-start = ((), (), s32[]{:S(2)}) async-start(), calls=%async_computation.4 | async-start | bytes 2359296 | tf_op jit(solution)/shard_map/all_gather | solution.py:293
  11.0 493.7 %all-gather.12.cloned.1.call-start = ((), (), s32[]{:S(2)}) async-start(), calls=%async_computation.5 | async-start | bytes 2359296 | tf_op jit(solution)/shard_map/all_gather | solution.py:295
  11.8 670.7 %all-gather.14.cloned.1.call-start = ((), (), s32[]{:S(2)}) async-start(), calls=%async_computation.6 | async-start | bytes 4718592 | tf_op jit(solution)/shard_map/all_gather | solution.py:296
  12.5 108.3 %copy-start.36 = (f32[2304]{0:T(1024)}, f32[2304]{0:T(1024)S(1)}, u32[]{:S(2)}) copy-start(f32[2304]{0:T(1024)S(1)} %get-tuple-element.502) | copy-start | bytes 27652
  12.5 108.3 %copy-start.38 = (f32[2304]{0:T(1024)}, f32[2304]{0:T(1024)S(1)}, u32[]{:S(2)}) copy-start(f32[2304]{0:T(1024)S(1)} %get-tuple-element.503) | copy-start | bytes 27652
  101.3 18.4 %collective-permute-start.2 = (bf16[3,2304]{1,0:T(4,128)(2,1)}, bf16[3,2304]{1,0:T(4,128)(2,1)}, u32[]{:S(2)}, u32[]{:S(2)}) collective-permute-start(bf16[3,2304]{1,0:T(4,128)(2,1)} %slice.205), channel_id=1, source_target_pairs={{0,1},{1,2},{2,3},{3,4},{4,5},{5,6},{6,7},{8,9},{9,10},{10,11},{11... | collective-permute-start | bytes 41480 | tf_op jit(solution)/shard_map/ppermute | solution.py:52
  134.0 5.0 collective-permute-start
  141.8 25.2 %collective-permute-start = (f32[32,64,128]{2,1,0:T(8,128)}, f32[32,64,128]{2,1,0:T(8,128)S(1)}, u32[]{:S(2)}, u32[]{:S(2)}) collective-permute-start(f32[32,64,128]{2,1,0:T(8,128)} %multiply_add_fusion.13), channel_id=1, source_target_pairs={{0,1},{1,2},{2,3},{3,4},{4,5},{5,6},{6,7},{8,9},{9,10},{10,11},{11... | collective-permute-start | bytes 3145736 | tf_op jit(solution)/shard_map/while/body/eval_jaxpr/ppermute | solution.py:52
  169.5 33.1 %collective-permute-start = (f32[32,64,128]{2,1,0:T(8,128)}, f32[32,64,128]{2,1,0:T(8,128)S(1)}, u32[]{:S(2)}, u32[]{:S(2)}) collective-permute-start(f32[32,64,128]{2,1,0:T(8,128)} %multiply_add_fusion.13), channel_id=1, source_target_pairs={{0,1},{1,2},{2,3},{3,4},{4,5},{5,6},{6,7},{8,9},{9,10},{10,11},{11... | collective-permute-start | bytes 3145736 | tf_op jit(solution)/shard_map/while/body/eval_jaxpr/ppermute | solution.py:52
  205.1 31.6 %collective-permute-start = (f32[32,64,128]{2,1,0:T(8,128)}, f32[32,64,128]{2,1,0:T(8,128)S(1)}, u32[]{:S(2)}, u32[]{:S(2)}) collective-permute-start(f32[32,64,128]{2,1,0:T(8,128)} %multiply_add_fusion.13), channel_id=1, source_target_pairs={{0,1},{1,2},{2,3},{3,4},{4,5},{5,6},{6,7},{8,9},{9,10},{10,11},{11... | collective-permute-start | bytes 3145736 | tf_op jit(solution)/shard_map/while/body/eval_jaxpr/ppermute | solution.py:52
  239.2 16.3 %collective-permute-start = (f32[32,64,128]{2,1,0:T(8,128)}, f32[32,64,128]{2,1,0:T(8,128)S(1)}, u32[]{:S(2)}, u32[]{:S(2)}) collective-permute-start(f32[32,64,128]{2,1,0:T(8,128)} %multiply_add_fusion.13), channel_id=1, source_target_pairs={{0,1},{1,2},{2,3},{3,4},{4,5},{5,6},{6,7},{8,9},{9,10},{10,11},{11... | collective-permute-start | bytes 3145736 | tf_op jit(solution)/shard_map/while/body/eval_jaxpr/ppermute | solution.py:52
  258.0 16.3 %collective-permute-start = (f32[32,64,128]{2,1,0:T(8,128)}, f32[32,64,128]{2,1,0:T(8,128)S(1)}, u32[]{:S(2)}, u32[]{:S(2)}) collective-permute-start(f32[32,64,128]{2,1,0:T(8,128)} %multiply_add_fusion.13), channel_id=1, source_target_pairs={{0,1},{1,2},{2,3},{3,4},{4,5},{5,6},{6,7},{8,9},{9,10},{10,11},{11... | collective-permute-start | bytes 3145736 | tf_op jit(solution)/shard_map/while/body/eval_jaxpr/ppermute | solution.py:52
  276.8 16.3 %collective-permute-start = (f32[32,64,128]{2,1,0:T(8,128)}, f32[32,64,128]{2,1,0:T(8,128)S(1)}, u32[]{:S(2)}, u32[]{:S(2)}) collective-permute-start(f32[32,64,128]{2,1,0:T(8,128)} %multiply_add_fusion.13), channel_id=1, source_target_pairs={{0,1},{1,2},{2,3},{3,4},{4,5},{5,6},{6,7},{8,9},{9,10},{10,11},{11... | collective-permute-start | bytes 3145736 | tf_op jit(solution)/shard_map/while/body/eval_jaxpr/ppermute | solution.py:52
  325.6 15.6 %collective-permute-start.1 = (bf16[32,64,128]{2,1,0:T(8,128)(2,1)}, bf16[32,64,128]{2,1,0:T(8,128)(2,1)}, u32[]{:S(2)}, u32[]{:S(2)}) collective-permute-start(bf16[32,64,128]{2,1,0:T(8,128)(2,1)} %fusion.145), channel_id=1, source_target_pairs={{1,0},{2,1},{3,2},{4,3},{5,4},{6,5},{7,6},{9,8},{10,9},{11,10},{12... | collective-permute-start | bytes 1572872 | tf_op jit(solution)/shard_map/while/body/eval_jaxpr/ppermute | solution.py:52
  344.6 11.4 %collective-permute-start.1 = (bf16[32,64,128]{2,1,0:T(8,128)(2,1)}, bf16[32,64,128]{2,1,0:T(8,128)(2,1)}, u32[]{:S(2)}, u32[]{:S(2)}) collective-permute-start(bf16[32,64,128]{2,1,0:T(8,128)(2,1)} %fusion.145), channel_id=1, source_target_pairs={{1,0},{2,1},{3,2},{4,3},{5,4},{6,5},{7,6},{9,8},{10,9},{11,10},{12... | collective-permute-start | bytes 1572872 | tf_op jit(solution)/shard_map/while/body/eval_jaxpr/ppermute | solution.py:52
  359.4 10.8 %collective-permute-start.1 = (bf16[32,64,128]{2,1,0:T(8,128)(2,1)}, bf16[32,64,128]{2,1,0:T(8,128)(2,1)}, u32[]{:S(2)}, u32[]{:S(2)}) collective-permute-start(bf16[32,64,128]{2,1,0:T(8,128)(2,1)} %fusion.145), channel_id=1, source_target_pairs={{1,0},{2,1},{3,2},{4,3},{5,4},{6,5},{7,6},{9,8},{10,9},{11,10},{12... | collective-permute-start | bytes 1572872 | tf_op jit(solution)/shard_map/while/body/eval_jaxpr/ppermute | solution.py:52
  373.6 10.8 %collective-permute-start.1 = (bf16[32,64,128]{2,1,0:T(8,128)(2,1)}, bf16[32,64,128]{2,1,0:T(8,128)(2,1)}, u32[]{:S(2)}, u32[]{:S(2)}) collective-permute-start(bf16[32,64,128]{2,1,0:T(8,128)(2,1)} %fusion.145), channel_id=1, source_target_pairs={{1,0},{2,1},{3,2},{4,3},{5,4},{6,5},{7,6},{9,8},{10,9},{11,10},{12... | collective-permute-start | bytes 1572872 | tf_op jit(solution)/shard_map/while/body/eval_jaxpr/ppermute | solution.py:52
  387.8 10.8 %collective-permute-start.1 = (bf16[32,64,128]{2,1,0:T(8,128)(2,1)}, bf16[32,64,128]{2,1,0:T(8,128)(2,1)}, u32[]{:S(2)}, u32[]{:S(2)}) collective-permute-start(bf16[32,64,128]{2,1,0:T(8,128)(2,1)} %fusion.145), channel_id=1, source_target_pairs={{1,0},{2,1},{3,2},{4,3},{5,4},{6,5},{7,6},{9,8},{10,9},{11,10},{12... | collective-permute-start | bytes 1572872 | tf_op jit(solution)/shard_map/while/body/eval_jaxpr/ppermute | solution.py:52
  402.0 10.8 %collective-permute-start.1 = (bf16[32,64,128]{2,1,0:T(8,128)(2,1)}, bf16[32,64,128]{2,1,0:T(8,128)(2,1)}, u32[]{:S(2)}, u32[]{:S(2)}) collective-permute-start(bf16[32,64,128]{2,1,0:T(8,128)(2,1)} %fusion.145), channel_id=1, source_target_pairs={{1,0},{2,1},{3,2},{4,3},{5,4},{6,5},{7,6},{9,8},{10,9},{11,10},{12... | collective-permute-start | bytes 1572872 | tf_op jit(solution)/shard_map/while/body/eval_jaxpr/ppermute | solution.py:52
  416.2 10.8 %collective-permute-start.1 = (bf16[32,64,128]{2,1,0:T(8,128)(2,1)}, bf16[32,64,128]{2,1,0:T(8,128)(2,1)}, u32[]{:S(2)}, u32[]{:S(2)}) collective-permute-start(bf16[32,64,128]{2,1,0:T(8,128)(2,1)} %fusion.145), channel_id=1, source_target_pairs={{1,0},{2,1},{3,2},{4,3},{5,4},{6,5},{7,6},{9,8},{10,9},{11,10},{12... | collective-permute-start | bytes 1572872 | tf_op jit(solution)/shard_map/while/body/eval_jaxpr/ppermute | solution.py:52
  484.0 10.1 %collective-permute-start.3 = (f32[3,2304]{1,0:T(4,128)}, f32[3,2304]{1,0:T(4,128)}, u32[]{:S(2)}, u32[]{:S(2)}) collective-permute-start(f32[3,2304]{1,0:T(4,128)} %pad_add_fusion.1), channel_id=1, source_target_pairs={{1,0},{2,1},{3,2},{4,3},{5,4},{6,5},{7,6},{9,8},{10,9},{11,10},{12... | collective-permute-start | bytes 82952 | tf_op jit(solution)/shard_map/ppermute | solution.py:52
  485.3 201.3 %reduce-scatter.7.cloned.1.call-start = ((), (), s32[]{:S(2)}) async-start(), calls=%async_computation.7 | async-start | bytes 1433600
  496.1 43.5 %collective-permute-start.4 = (bf16[128,4384]{0,1:T(8,128)(2,1)S(1)}, bf16[128,4384]{0,1:T(8,128)(2,1)}, u32[]{:S(2)}, u32[]{:S(2)}) collective-permute-start(bf16[128,4384]{0,1:T(8,128)(2,1)S(1)} %copy.233), channel_id=1, source_target_pairs={{0,1},{1,2},{2,3},{3,4},{4,5},{5,6},{6,7},{7,0},{8,9},{9,10},{10,1... | collective-permute-start | bytes 3366920 | tf_op jit(solution)/shard_map/ppermute | solution.py:37
  498.8 49.8 %collective-permute-start.5 = (bf16[128,4384]{0,1:T(8,128)(2,1)S(1)}, bf16[128,4384]{0,1:T(8,128)(2,1)}, u32[]{:S(2)}, u32[]{:S(2)}) collective-permute-start(bf16[128,4384]{0,1:T(8,128)(2,1)S(1)} %copy.233), channel_id=1, source_target_pairs={{0,7},{1,0},{2,1},{3,2},{4,3},{5,4},{6,5},{7,6},{8,15},{9,8},{10,9... | collective-permute-start | bytes 3366920 | tf_op jit(solution)/shard_map/ppermute | solution.py:42
  539.5 36.1 %collective-permute-start.6 = (bf16[128,4384]{0,1:T(8,128)(2,1)}, bf16[128,4384]{0,1:T(8,128)(2,1)S(1)}, u32[]{:S(2)}, u32[]{:S(2)}) collective-permute-start(bf16[128,4384]{0,1:T(8,128)(2,1)} %collective-permute-done.4), channel_id=1, source_target_pairs={{0,1},{1,2},{2,3},{3,4},{4,5},{5,6},{6,7},{7,0},{8,9},{9,10},{10,1... | collective-permute-start | bytes 3366920 | tf_op jit(solution)/shard_map/ppermute | solution.py:37
  548.6 33.5 %collective-permute-start.7 = (bf16[128,4384]{0,1:T(8,128)(2,1)}, bf16[128,4384]{0,1:T(8,128)(2,1)S(1)}, u32[]{:S(2)}, u32[]{:S(2)}) collective-permute-start(bf16[128,4384]{0,1:T(8,128)(2,1)} %collective-permute-done.5), channel_id=1, source_target_pairs={{0,7},{1,0},{2,1},{3,2},{4,3},{5,4},{6,5},{7,6},{8,15},{9,8},{10,9... | collective-permute-start | bytes 3366920 | tf_op jit(solution)/shard_map/ppermute | solution.py:42
  575.6 23.5 %collective-permute-start.8 = (bf16[128,4384]{0,1:T(8,128)(2,1)S(1)}, bf16[128,4384]{0,1:T(8,128)(2,1)S(1)}, u32[]{:S(2)}, u32[]{:S(2)}) collective-permute-start(bf16[128,4384]{0,1:T(8,128)(2,1)S(1)} %collective-permute-done.6), channel_id=1, source_target_pairs={{0,1},{1,2},{2,3},{3,4},{4,5},{5,6},{6,7},{7,0},{8,9},{9,10},{10,1... | collective-permute-start | bytes 3366920 | tf_op jit(solution)/shard_map/ppermute | solution.py:37
  582.1 25.9 %collective-permute-start.9 = (bf16[128,4384]{0,1:T(8,128)(2,1)S(1)}, bf16[128,4384]{0,1:T(8,128)(2,1)S(1)}, u32[]{:S(2)}, u32[]{:S(2)}) collective-permute-start(bf16[128,4384]{0,1:T(8,128)(2,1)S(1)} %collective-permute-done.7), channel_id=1, source_target_pairs={{0,7},{1,0},{2,1},{3,2},{4,3},{5,4},{6,5},{7,6},{8,15},{9,8},{10,9... | collective-permute-start | bytes 3366920 | tf_op jit(solution)/shard_map/ppermute | solution.py:42
  599.0 20.8 %collective-permute-start.10 = (bf16[128,4384]{0,1:T(8,128)(2,1)S(1)}, bf16[128,4384]{0,1:T(8,128)(2,1)S(1)}, u32[]{:S(2)}, u32[]{:S(2)}) collective-permute-start(bf16[128,4384]{0,1:T(8,128)(2,1)S(1)} %collective-permute-done.8), channel_id=1, source_target_pairs={{0,1},{1,2},{2,3},{3,4},{4,5},{5,6},{6,7},{7,0},{8,9},{9,10},{10,1... | collective-permute-start | bytes 3366920 | tf_op jit(solution)/shard_map/ppermute | solution.py:37
  625.3 86.8 %reduce-scatter.9.cloned.1.call-start = ((), (), s32[]{:S(2)}) async-start(), calls=%async_computation.8 | async-start | bytes 655360
  (77 other events, 971.4 us)
Sparse Core Ops, SparseCore 0:
  11.4 82.9 all-gather.5
  98.1 60.2 all-gather.7
  160.5 34.3 all-gather.9
  197.0 34.3 all-gather.11
  485.4 81.0 all-gather.13
  625.4 35.7 reduce-scatter.6
  686.6 25.4 reduce-scatter.8
